TPU v7x, 256 devices: a whole 4x4x8 slice. The times are simulated.
256 devices in a mesh: dp: 64 (over x, z, core), rep: 4 (over y).
Axes of the slice: x: 4, y: 4, z: 8, core: 2. Of those that a mesh axis runs over, the one named last changes fastest.
Arguments:
- frames_in: bfloat16 [4, 57344, 1536], P('rep', 'dp')
- lengths: int32 [4, 64, 4], P('rep', 'dp'), may hold values from 1 to 893, as said below
- norm_gain: float32 [1536], replicated, may hold values from 0.5 to 1.5
- norm_bias: float32 [1536], replicated, may hold values from -2 to 2
- w_in: bfloat16 [1536, 3072], P(('dp', 'rep')), may hold values from -0.15625 to 0.15625
- kernel: float32 [31, 1536], replicated, may hold values from -1 to 1
- batch_gain: float32 [1536], replicated, may hold values from 0.5 to 1.5
- batch_bias: float32 [1536], replicated, may hold values from -3 to 3
- w_out: bfloat16 [1536, 1536], P(('dp', 'rep')), may hold values from -0.15625 to 0.15625
Outputs:
- frames_out: bfloat16 [4, 57344, 1536], P('rep', 'dp')
Inputs may be any that keep to these rules, and one draw needn't show every extreme that they name: `lengths`: for each rep index, the devices 2k and 2k + 1 of dp hold 1024 frames together, so each rep index holds 512 frames for each of its dp devices; a device holds at most 896 frames, and some device of every rep index holds exactly 896.
All inputs are finite; a program needn't handle non-finite values.
Results may differ from a plain program's by a relative error of at most 0.0038.
Values may be sent and summed in bfloat16 or wider, within the bound.
A program may use at most 128 MiB of HBM per device.

v0:
```python
import jax
import jax.numpy as jnp
from jax import lax
from jax.sharding import PartitionSpec as P

FR_DEV = 512
EPSILON = 1e-05


def layer_norm(frames, norm_gain, norm_bias):
    values = frames.astype(jnp.float32)
    average = jnp.mean(values, axis=-1, keepdims=True)
    centred = values - average
    spread = jnp.mean(centred * centred, axis=-1, keepdims=True)
    return centred * lax.rsqrt(spread + EPSILON) * norm_gain + norm_bias


def depthwise(gated, labels, kernel):
    half_kernel = kernel.shape[0] // 2
    length_rows = gated.shape[0]
    padded = jnp.pad(gated, ((half_kernel, half_kernel), (0, 0)))
    padded_labels = jnp.pad(labels, (half_kernel, half_kernel), constant_values=-1)
    summed = jnp.zeros(gated.shape, jnp.float32)
    for offset in range(kernel.shape[0]):
        shared = padded_labels[offset : offset + length_rows] == labels
        contribution = jnp.where(
            shared[:, None], padded[offset : offset + length_rows].astype(jnp.float32), 0.0
        )
        summed = summed + contribution * kernel[offset]
    return summed


def project_in(normed, weight_rows):
    return jnp.dot(normed, weight_rows, preferred_element_type=jnp.float32)


def project_out(active, weight_rows):
    return jnp.dot(active, weight_rows, preferred_element_type=jnp.float32)


def on_device(
    frames_in, lengths, norm_gain, norm_bias, w_in, kernel, batch_gain, batch_bias, w_out
):
    local_frames = frames_in[0]
    local_lengths = lengths[0, 0]
    capacity = local_frames.shape[0]
    features = local_frames.shape[1]
    total_count = lax.axis_size("dp") * lax.axis_size("rep") * FR_DEV
    grouped = (w_in, w_out)
    grouped = (
        lax.all_gather(w_in, ("dp", "rep"), axis=0, tiled=True),
        lax.all_gather(w_out, ("dp", "rep"), axis=0, tiled=True),
    )
    rows_here = jnp.arange(capacity, dtype=jnp.int32)
    local_load = jnp.sum(local_lengths)
    bounds = jnp.cumsum(local_lengths)
    labels = jnp.sum((rows_here[:, None] >= bounds[None, :]).astype(jnp.int32), axis=1)
    row_weight = (rows_here < local_load).astype(jnp.float32)[:, None]
    normed = layer_norm(local_frames, norm_gain, norm_bias).astype(jnp.bfloat16)
    projected = project_in(normed, grouped[0])
    gated = (projected[:, :features] * jax.nn.sigmoid(projected[:, features:])).astype(jnp.bfloat16)
    convolved = depthwise(gated, labels, kernel)
    average = lax.psum(jnp.sum(convolved * row_weight, axis=0), ("dp", "rep")) / total_count
    centred = convolved - average
    spread = lax.psum(jnp.sum(centred * centred * row_weight, axis=0), ("dp", "rep")) / total_count
    scaled = centred * lax.rsqrt(spread + EPSILON) * batch_gain + batch_bias
    active = jax.nn.silu(scaled).astype(jnp.bfloat16)
    branch = project_out(active, grouped[1])
    mixed = (local_frames.astype(jnp.float32) + branch).astype(jnp.bfloat16)
    result = jnp.where(rows_here[:, None] < local_load, mixed, jnp.zeros_like(mixed))
    return result[None]


def solution(mesh):
    placed = (
        P("rep", "dp", None),
        P("rep", "dp", None),
        P(),
        P(),
        P(("dp", "rep"), None),
        P(),
        P(),
        P(),
        P(("dp", "rep"), None),
    )
    return jax.shard_map(
        on_device, mesh=mesh, in_specs=placed, out_specs=P("rep", "dp", None), check_vma=False
    )
```

profile of v0, /device:TPU:1, one launch (start us, length us, event | category | flops | bytes accessed | tf_op | source)
XLA Modules:
  0.0 487.7 jit_solution(4124133330554323458)
XLA Ops:
  6.5 0.0 all-gather.7.cloned.1.call-start
  6.5 0.7 all-gather.7.cloned.1.call-update
  7.3 0.0 all-gather.5.cloned.1.call-start
  7.3 0.7 all-gather.5.cloned.1.call-update
  8.0 1.3 reduce_sum.54
  9.3 0.8 reduce-window.8
  10.1 0.6 iota_compare_fusion.1
  10.8 0.7 fusion.26
  11.4 0.1 convert_reduce_fusion.1
  11.5 1.5 slice_reduce_fusion.29
  13.0 1.8 slice_reduce_fusion.30
  14.9 0.1 slice_compare_fusion.26
  14.9 2.2 convert_reduce_fusion
  17.2 2.6 fusion.4
  19.8 0.1 slice_compare_fusion.29
  19.9 0.1 slice_compare_fusion.28
  20.0 0.1 slice_compare_fusion.27
  20.1 111.2 %all-gather.7.cloned.1.call-done = bf16[256,6,1536]{2,1,0:T(8,128)(2,1)} async-done(((bf16[1,6,1536]{2,1,0:T(8,128)(2,1)}), bf16[256,6,1536]{2,1,0:T(8,128)(2,1)}) %all-gather.7.cloned.1.call-update) | async-done | bytes 4718608 | tf_op jit(solution)/shard_map/all_gather | solution.py:52
  131.3 8.5 %reshape.87 = bf16[1536,1536]{1,0:T(8,128)(2,1)} reshape(bf16[256,6,1536]{2,1,0:T(8,128)(2,1)} %all-gather.7.cloned.1.call-done) | data formatting | bytes 9437184
  139.8 113.5 %all-gather.5.cloned.1.call-done = bf16[256,6,3072]{2,1,0:T(8,128)(2,1)} async-done(((bf16[1,6,3072]{2,1,0:T(8,128)(2,1)}), bf16[256,6,3072]{2,1,0:T(8,128)(2,1)}) %all-gather.5.cloned.1.call-update) | async-done | bytes 9437200 | tf_op jit(solution)/shard_map/all_gather | solution.py:51
  253.3 14.2 %reshape.85 = bf16[1536,3072]{1,0:T(8,128)(2,1)} reshape(bf16[256,6,3072]{2,1,0:T(8,128)(2,1)} %all-gather.5.cloned.1.call-done) | data formatting | bytes 18874368
  267.5 0.0 copy-done
  267.5 0.0 copy-done.2
  267.5 11.3 %fusion.16 = f32[896,3072]{1,0:T(8,128)S(1)} fusion(bf16[1536,3072]{1,0:T(8,128)(2,1)} %reshape.85, bf16[1,896,1536]{2,1,0:T(8,128)(2,1)S(1)} %copy-done, f32[1536]{0:T(1024)S(1)} %copy-done.2, f32[1536]{0:T(1024)S(1)} %copy-done.3, f32[896]{0:T(1024)S(1)} %add_rsqrt_fusion.1, f32[896]{0:T(1024)S(1)} %broadcast_multiply_fusion.1), kind=kOutput, calls=%fused_computation.23 | convolution fusion | flops 8463974400 | bytes 23219200 | tf_op jit(solution)/shard_map/dot_general | solution.py:34
  278.8 1.5 fusion.13
  280.4 0.0 copy-start.4
  280.4 0.0 copy-start.5
  280.4 38.3 %multiply_reduce_fusion.1 = (f32[1536]{0:T(1024)S(1)}, f32[896,1536]{1,0:T(8,128)}) fusion(f32[896]{0:T(1024)S(1)} %fusion.26, f32[1536]{0:T(1024)S(1)} %get-tuple-element.34, pred[896]{0:T(1024)(128)(4,1)S(1)} %get-tuple-element.67, f32[1536]{0:T(1024)S(1)} %get-tuple-element.35, pred[896]{0:T(1024)(128)(4,1)S(1)} %get-tuple-element.39, ...), kind=kLoop, calls=%fused_computation.18 | loop fusion | flops 170654208 | bytes 8484608 | tf_op jit(solution)/shard_map/reduce_sum | solution.py:63
  318.7 74.8 %psum.14 = f32[1536]{0:T(1024)S(1)} all-reduce(f32[1536]{0:T(1024)S(1)} %get-tuple-element.36), channel_id=1, replica_groups=mesh['dp'=64,'rep'=4] {'dp','rep'}, use_global_device_ids=true, to_apply=%region_6.7 | all-reduce | flops 1536 | bytes 12288 | tf_op jit(solution)/shard_map/psum | solution.py:63
  393.5 3.3 multiply_reduce_fusion
  396.8 73.6 %psum.15 = f32[1536]{0:T(1024)S(1)} all-reduce(f32[1536]{0:T(1024)S(1)} %multiply_reduce_fusion), channel_id=1, replica_groups=mesh['dp'=64,'rep'=4] {'dp','rep'}, use_global_device_ids=true, to_apply=%region_8.9 | all-reduce | flops 1536 | bytes 12288 | tf_op jit(solution)/shard_map/psum | solution.py:65
  470.4 10.4 %fusion.15 = bf16[1,896,1536]{2,1,0:T(8,128)(2,1)} fusion(bf16[1536,1536]{1,0:T(8,128)(2,1)} %reshape.87, bf16[1,896,1536]{2,1,0:T(8,128)(2,1)S(1)} %copy-done.1, f32[896,1536]{1,0:T(8,128)} %get-tuple-element.37, f32[1536]{0:T(1024)S(1)} %copy-done.4, f32[1536]{0:T(1024)S(1)} %copy-done.5, f32[1536]{0:T(1024)S(1)} %add_rsqrt_fusion, ...), kind=kOutput, calls=%fused_computation.22 | convolution fusion | flops 4245749760 | bytes 15754112 | tf_op jit(solution)/shard_map/dot_general | solution.py:38
  (12 shorter events, 0.0 us)
Async XLA Ops:
  6.5 124.8 %all-gather.7.cloned.1.call-start = ((), (), s32[]{:S(2)}) async-start(), calls=%async_computation.1 | async-start | bytes 6316032 | tf_op jit(solution)/shard_map/all_gather | solution.py:52
  7.3 246.1 %all-gather.5.cloned.1.call-start = ((), (), s32[]{:S(2)}) async-start(), calls=%async_computation | async-start | bytes 12632064 | tf_op jit(solution)/shard_map/all_gather | solution.py:51
  139.8 127.7 %copy-start = (bf16[1,896,1536]{2,1,0:T(8,128)(2,1)S(1)}, bf16[1,896,1536]{2,1,0:T(8,128)(2,1)}, u32[]{:S(2)}) copy-start(bf16[1,896,1536]{2,1,0:T(8,128)(2,1)} %param.9) | copy-start | bytes 8257540
  139.8 127.7 %copy-start.2 = (f32[1536]{0:T(1024)S(1)}, f32[1536]{0:T(1024)}, u32[]{:S(2)}) copy-start(f32[1536]{0:T(1024)} %param.12) | copy-start | bytes 18436
  139.8 127.7 %copy-start.3 = (f32[1536]{0:T(1024)S(1)}, f32[1536]{0:T(1024)}, u32[]{:S(2)}) copy-start(f32[1536]{0:T(1024)} %param.11) | copy-start | bytes 18436
  280.4 190.1 %copy-start.4 = (f32[1536]{0:T(1024)S(1)}, f32[1536]{0:T(1024)}, u32[]{:S(2)}) copy-start(f32[1536]{0:T(1024)} %param.16) | copy-start | bytes 18436
  280.4 190.1 %copy-start.5 = (f32[1536]{0:T(1024)S(1)}, f32[1536]{0:T(1024)}, u32[]{:S(2)}) copy-start(f32[1536]{0:T(1024)} %param.15) | copy-start | bytes 18436
  318.7 151.7 %copy-start.1 = (bf16[1,896,1536]{2,1,0:T(8,128)(2,1)S(1)}, bf16[1,896,1536]{2,1,0:T(8,128)(2,1)}, u32[]{:S(2)}) copy-start(bf16[1,896,1536]{2,1,0:T(8,128)(2,1)} %param.9) | copy-start | bytes 8257540
Sparse Core Ops, SparseCore 0:
  11.2 120.0 all-gather.6
  135.1 118.1 all-gather.4
where the time goes:
time: 489 us; the launch traced here: 488 us
  waiting for transfers between devices  226 us (46%)
  blocking collectives  148 us (30%)
  other arithmetic  51.8 us (11%)
  local copies, waits for them, and re-layouts  26 us (5%)
  matrix products  21.8 us (4%)
  between operations  13.5 us (3%)
    all_gather x1, waiting for transfers between devices, on_device(): lax.all_gather(w_in, ('dp', 'rep'), axis=0, tiled=True)  114 us
    all_gather x1, waiting for transfers between devices, on_device(): lax.all_gather(w_out, ('dp', 'rep'), axis=0, tiled=True)  111 us
    psum x1, blocking collectives, on_device(): lax.psum(jnp.sum(convolved * row_weight, axis=0), ('dp', 'rep'))  74.8 us
    psum x1, blocking collectives, on_device(): lax.psum(jnp.sum(centred * centred * row_weight, axis=0), ('dp', 'rep'))  73.6 us
    reduce_sum x1, other arithmetic, on_device(): jnp.sum(convolved * row_weight, axis=0)  38.3 us
    unnamed x14, local copies, waits for them, and re-layouts  22.6 us
    dot_general x1, matrix products, project_in(): return jnp.dot(normed, weight_rows, preferred_element_type=jnp.float32)  11.3 us
    dot_general x1, matrix products, project_out(): return jnp.dot(active, weight_rows, preferred_element_type=jnp.float32)  10.4 us
  transfers between devices with their start and end apart: 2, of which 2 were waited for; matrix products, arithmetic and copies ran while one was open for 4% of the time, Pallas kernels for 0%

commit v1 on v0

--- a/solution.py
+++ b/solution.py
@@ -5,6 +5,11 @@
 
 FR_DEV = 512
 EPSILON = 1e-05
+
+
+def axis_by_axis(x, axis_one, axis_two):
+    half = lax.psum(x, axis_one)
+    return lax.psum(half, axis_two)
 
 
 def layer_norm(frames, norm_gain, norm_bias):
@@ -62,7 +67,9 @@
     convolved = depthwise(gated, labels, kernel)
     average = lax.psum(jnp.sum(convolved * row_weight, axis=0), ("dp", "rep")) / total_count
     centred = convolved - average
-    spread = lax.psum(jnp.sum(centred * centred * row_weight, axis=0), ("dp", "rep")) / total_count
+    spread = (
+        axis_by_axis(jnp.sum(centred * centred * row_weight, axis=0), "dp", "rep") / total_count
+    )
     scaled = centred * lax.rsqrt(spread + EPSILON) * batch_gain + batch_bias
     active = jax.nn.silu(scaled).astype(jnp.bfloat16)
     branch = project_out(active, grouped[1])

time: 489 us -> 551 us (1.13)
  blocking collectives: 148 us -> 209 us
    psum x1 -> x2, blocking collectives: 73.6 us -> 135 us  [the longest x1 126 us: axis_by_axis(): half = lax.psum(x, axis_one)]
where the time goes in v1:
time: 551 us; the launch traced here: 549 us
  waiting for transfers between devices  226 us (41%)
  blocking collectives  209 us (38%)
  other arithmetic  51.8 us (9%)
  local copies, waits for them, and re-layouts  26 us (5%)
  matrix products  21.8 us (4%)
  between operations  13.5 us (2%)
    psum x1, blocking collectives, axis_by_axis(): half = lax.psum(x, axis_one)  126 us
    all_gather x1, waiting for transfers between devices, on_device(): lax.all_gather(w_in, ('dp', 'rep'), axis=0, tiled=True)  114 us
    all_gather x1, waiting for transfers between devices, on_device(): lax.all_gather(w_out, ('dp', 'rep'), axis=0, tiled=True)  111 us
    psum x1, blocking collectives, on_device(): lax.psum(jnp.sum(convolved * row_weight, axis=0), ('dp', 'rep'))  74.8 us
    reduce_sum x1, other arithmetic, on_device(): jnp.sum(convolved * row_weight, axis=0)  38.3 us
    unnamed x14, local copies, waits for them, and re-layouts  22.6 us
    dot_general x1, matrix products, project_in(): return jnp.dot(normed, weight_rows, preferred_element_type=jnp.float32)  11.3 us
  transfers between devices with their start and end apart: 2, of which 2 were waited for; matrix products, arithmetic and copies ran while one was open for 4% of the time, Pallas kernels for 0%

profile of v1, /device:TPU:1, one launch (start us, length us, event | category | flops | bytes accessed | tf_op | source)
XLA Modules:
  0.0 548.6 jit_solution(4188371844213610456)
XLA Ops:
  6.5 0.7 all-gather.7.cloned.1.call-update
  7.3 0.0 all-gather.5.cloned.1.call-start
  7.3 0.7 all-gather.5.cloned.1.call-update
  8.0 1.3 reduce_sum.54
  9.3 0.8 reduce-window.8
  10.1 0.6 iota_compare_fusion.1
  10.8 0.7 fusion.26
  11.4 0.1 convert_reduce_fusion.1
  11.5 1.5 slice_reduce_fusion.29
  13.0 1.8 slice_reduce_fusion.30
  14.9 0.1 slice_compare_fusion.26
  14.9 2.2 convert_reduce_fusion
  17.2 2.6 fusion.4
  19.8 0.1 slice_compare_fusion.29
  19.9 0.1 slice_compare_fusion.28
  20.0 0.1 slice_compare_fusion.27
  20.1 111.2 %all-gather.7.cloned.1.call-done = bf16[256,6,1536]{2,1,0:T(8,128)(2,1)} async-done(((bf16[1,6,1536]{2,1,0:T(8,128)(2,1)}), bf16[256,6,1536]{2,1,0:T(8,128)(2,1)}) %all-gather.7.cloned.1.call-update) | async-done | bytes 4718608 | tf_op jit(solution)/shard_map/all_gather | solution.py:57
  131.3 8.5 %reshape.87 = bf16[1536,1536]{1,0:T(8,128)(2,1)} reshape(bf16[256,6,1536]{2,1,0:T(8,128)(2,1)} %all-gather.7.cloned.1.call-done) | data formatting | bytes 9437184
  139.8 113.5 %all-gather.5.cloned.1.call-done = bf16[256,6,3072]{2,1,0:T(8,128)(2,1)} async-done(((bf16[1,6,3072]{2,1,0:T(8,128)(2,1)}), bf16[256,6,3072]{2,1,0:T(8,128)(2,1)}) %all-gather.5.cloned.1.call-update) | async-done | bytes 9437200 | tf_op jit(solution)/shard_map/all_gather | solution.py:56
  253.3 14.2 %reshape.85 = bf16[1536,3072]{1,0:T(8,128)(2,1)} reshape(bf16[256,6,3072]{2,1,0:T(8,128)(2,1)} %all-gather.5.cloned.1.call-done) | data formatting | bytes 18874368
  267.5 11.3 %fusion.16 = f32[896,3072]{1,0:T(8,128)S(1)} fusion(bf16[1536,3072]{1,0:T(8,128)(2,1)} %reshape.85, bf16[1,896,1536]{2,1,0:T(8,128)(2,1)S(1)} %copy-done, f32[1536]{0:T(1024)S(1)} %copy-done.2, f32[1536]{0:T(1024)S(1)} %copy-done.3, f32[896]{0:T(1024)S(1)} %add_rsqrt_fusion.1, f32[896]{0:T(1024)S(1)} %broadcast_multiply_fusion.1), kind=kOutput, calls=%fused_computation.23 | convolution fusion | flops 8463974400 | bytes 23219200 | tf_op jit(solution)/shard_map/dot_general | solution.py:39
  278.8 1.5 fusion.13
  280.4 0.0 copy-start.4
  280.4 0.0 copy-start.5
  280.4 38.3 %multiply_reduce_fusion.1 = (f32[1536]{0:T(1024)S(1)}, f32[896,1536]{1,0:T(8,128)}) fusion(f32[896]{0:T(1024)S(1)} %fusion.26, f32[1536]{0:T(1024)S(1)} %get-tuple-element.34, pred[896]{0:T(1024)(128)(4,1)S(1)} %get-tuple-element.67, f32[1536]{0:T(1024)S(1)} %get-tuple-element.35, pred[896]{0:T(1024)(128)(4,1)S(1)} %get-tuple-element.39, ...), kind=kLoop, calls=%fused_computation.18 | loop fusion | flops 170654208 | bytes 8484608 | tf_op jit(solution)/shard_map/reduce_sum | solution.py:68
  318.7 74.8 %psum.21 = f32[1536]{0:T(1024)S(1)} all-reduce(f32[1536]{0:T(1024)S(1)} %get-tuple-element.36), channel_id=1, replica_groups=mesh['dp'=64,'rep'=4] {'dp','rep'}, use_global_device_ids=true, to_apply=%region_6.7 | all-reduce | flops 1536 | bytes 12288 | tf_op jit(solution)/shard_map/psum | solution.py:68
  393.5 3.3 multiply_reduce_fusion
  396.8 126.1 %psum.22 = f32[1536]{0:T(1024)S(1)} all-reduce(f32[1536]{0:T(1024)S(1)} %multiply_reduce_fusion), channel_id=1, replica_groups=mesh['dp'=64,'rep'=4] {'dp'}, use_global_device_ids=true, to_apply=%region_8.9 | all-reduce | flops 1536 | bytes 12288 | tf_op jit(solution)/shard_map/psum | solution.py:11
  522.9 8.4 %psum.23 = f32[1536]{0:T(1024)S(1)} all-reduce(f32[1536]{0:T(1024)S(1)} %psum.22), channel_id=1, replica_groups=mesh['dp'=64,'rep'=4] {'rep'}, use_global_device_ids=true, to_apply=%region_9.10 | all-reduce | flops 1536 | bytes 12288 | tf_op jit(solution)/shard_map/psum | solution.py:12
  531.3 0.0 copy-done.4
  531.3 0.0 copy-done.5
  531.4 10.4 %fusion.15 = bf16[1,896,1536]{2,1,0:T(8,128)(2,1)} fusion(bf16[1536,1536]{1,0:T(8,128)(2,1)} %reshape.87, bf16[1,896,1536]{2,1,0:T(8,128)(2,1)S(1)} %copy-done.1, f32[896,1536]{1,0:T(8,128)} %get-tuple-element.37, f32[1536]{0:T(1024)S(1)} %copy-done.4, f32[1536]{0:T(1024)S(1)} %copy-done.5, f32[1536]{0:T(1024)S(1)} %add_rsqrt_fusion, ...), kind=kOutput, calls=%fused_computation.22 | convolution fusion | flops 4245749760 | bytes 15754112 | tf_op jit(solution)/shard_map/dot_general | solution.py:43
  (13 shorter events, 0.0 us)
Async XLA Ops:
  6.5 124.8 %all-gather.7.cloned.1.call-start = ((), (), s32[]{:S(2)}) async-start(), calls=%async_computation.1 | async-start | bytes 6316032 | tf_op jit(solution)/shard_map/all_gather | solution.py:57
  7.3 246.1 %all-gather.5.cloned.1.call-start = ((), (), s32[]{:S(2)}) async-start(), calls=%async_computation | async-start | bytes 12632064 | tf_op jit(solution)/shard_map/all_gather | solution.py:56
  139.8 127.7 %copy-start = (bf16[1,896,1536]{2,1,0:T(8,128)(2,1)S(1)}, bf16[1,896,1536]{2,1,0:T(8,128)(2,1)}, u32[]{:S(2)}) copy-start(bf16[1,896,1536]{2,1,0:T(8,128)(2,1)} %param.9) | copy-start | bytes 8257540
  139.8 127.7 %copy-start.2 = (f32[1536]{0:T(1024)S(1)}, f32[1536]{0:T(1024)}, u32[]{:S(2)}) copy-start(f32[1536]{0:T(1024)} %param.12) | copy-start | bytes 18436
  139.8 127.7 %copy-start.3 = (f32[1536]{0:T(1024)S(1)}, f32[1536]{0:T(1024)}, u32[]{:S(2)}) copy-start(f32[1536]{0:T(1024)} %param.11) | copy-start | bytes 18436
  280.4 251.0 %copy-start.4 = (f32[1536]{0:T(1024)S(1)}, f32[1536]{0:T(1024)}, u32[]{:S(2)}) copy-start(f32[1536]{0:T(1024)} %param.16) | copy-start | bytes 18436
  280.4 251.0 %copy-start.5 = (f32[1536]{0:T(1024)S(1)}, f32[1536]{0:T(1024)}, u32[]{:S(2)}) copy-start(f32[1536]{0:T(1024)} %param.15) | copy-start | bytes 18436
  318.7 212.6 %copy-start.1 = (bf16[1,896,1536]{2,1,0:T(8,128)(2,1)S(1)}, bf16[1,896,1536]{2,1,0:T(8,128)(2,1)}, u32[]{:S(2)}) copy-start(bf16[1,896,1536]{2,1,0:T(8,128)(2,1)} %param.9) | copy-start | bytes 8257540
Sparse Core Ops, SparseCore 0:
  11.2 120.0 all-gather.6
  135.1 118.1 all-gather.4
